TPU v7x, 512 devices: a whole 4x4x16 slice. The times are simulated.
512 devices in a mesh: row: 8 (over x, core), col: 16 (over z), depth: 4 (over y).
Axes of the slice: x: 4, y: 4, z: 16, core: 2. Of those that a mesh axis runs over, the one named last changes fastest.
Arguments:
- k_parts: bfloat16 [2, 4096, 4096], P(None, 'row', 'col'), as said below
- p_parts: bfloat16 [2, 4096, 4096], P(None, 'row', 'col'), as said below
- k_mask: int32 [64, 64], P('row', 'col'), may hold values from 0 to 1, as said below
- p_mask: int32 [64, 64], P('row', 'col'), may hold values from 0 to 1, as said below
- atoms: int32 [64], replicated, may hold values from 0 to 15, as said below
- classes: int32 [16, 16], replicated, may hold values from 0 to 3
- rates: float32 [4], replicated, may hold values from 0.5 to 8
Outputs:
- derivative: float32 [2, 4096, 4096], P(None, ('row', 'depth'), 'col')
Inputs may be any that keep to these rules, and one draw needn't show every extreme that they name: k_parts[0] is symmetric and k_parts[1] antisymmetric, so the Kohn-Sham matrix is Hermitian. p_parts[0] is symmetric and p_parts[1] antisymmetric, so the density matrix is Hermitian. `k_mask`: symmetric; every diagonal tile is kept; each tile row keeps a band of tiles around the diagonal of its own half-width, from 0 to 16 tiles, besides scattered tiles further away. `p_mask`: symmetric; every diagonal tile is kept; each tile row keeps a band of tiles around the diagonal of its own half-width, from 0 to 16 tiles, besides scattered tiles further away. `atoms`: never falling along the tiles; every atom block holds at least one tile.
All inputs are finite; a program needn't handle non-finite values.
Results may differ from a plain program's by a relative error of at most 0.0003.
Values may be sent and summed in bfloat16 or wider, within the bound.
A program may use at most 64 MiB of HBM per device.

v0:
```python
import jax
import jax.numpy as jnp
from jax import lax
from jax.sharding import PartitionSpec as P

TILE = 64


def expand_mask(mask, tile, dtype):
    rows_t, cols_t = mask.shape
    grid = jnp.broadcast_to(mask[:, None, :, None], (rows_t, tile, cols_t, tile))
    return grid.reshape(rows_t * tile, cols_t * tile).astype(dtype)


def commute(k_rows, p_rows, k_cols, p_cols):
    left = jnp.concatenate((k_rows[0], k_rows[1], p_rows[0], p_rows[1]), axis=1)
    right = jnp.concatenate(
        (
            jnp.concatenate((p_cols[0], p_cols[1]), axis=1),
            jnp.concatenate((-p_cols[1], p_cols[0]), axis=1),
            jnp.concatenate((-k_cols[0], -k_cols[1]), axis=1),
            jnp.concatenate((k_cols[1], -k_cols[0]), axis=1),
        ),
        axis=0,
    )
    return jnp.dot(left, right, preferred_element_type=jnp.float32)


def make_fold(k_strip, p_strip, pieces):
    k_piece, p_piece = pieces
    return commute(k_strip, p_strip, k_piece, p_piece)


def body(k_parts, p_parts, k_mask, p_mask, atoms, classes, rates):
    k_local = k_parts * expand_mask(k_mask, TILE, jnp.bfloat16)[None]
    p_local = p_parts * expand_mask(p_mask, TILE, jnp.bfloat16)[None]
    rows_here = k_local.shape[1]
    cols_here = k_local.shape[2]
    depth = lax.axis_size("depth")
    layer = lax.axis_index("depth")
    out_rows = rows_here // depth
    k_strip = lax.dynamic_slice_in_dim(k_local, layer * out_rows, out_rows, 1)
    p_strip = lax.dynamic_slice_in_dim(p_local, layer * out_rows, out_rows, 1)
    k_strip, p_strip = (
        lax.all_gather(k_strip, "col", axis=2, tiled=True),
        lax.all_gather(p_strip, "col", axis=2, tiled=True),
    )
    total = make_fold(
        k_strip,
        p_strip,
        (
            lax.all_gather(k_local, "row", axis=1, tiled=True),
            lax.all_gather(p_local, "row", axis=1, tiled=True),
        ),
    )
    z_real = total[:, :cols_here]
    z_imag = total[:, cols_here:]
    grid_row = lax.axis_index("row") * depth + layer
    row_tiles = out_rows // TILE
    col_tiles = cols_here // TILE
    atom_rows = lax.dynamic_slice_in_dim(atoms, grid_row * row_tiles, row_tiles)
    atom_cols = lax.dynamic_slice_in_dim(atoms, lax.axis_index("col") * col_tiles, col_tiles)
    blocks = classes.shape[0]
    levels = rates.shape[0]
    block_ids = jnp.arange(blocks, dtype=jnp.int32)
    hot_rows = (atom_rows[:, None] == block_ids[None, :]).astype(jnp.float32)
    hot_cols = (atom_cols[:, None] == block_ids[None, :]).astype(jnp.float32)
    kinds = jnp.dot(
        jnp.dot(hot_rows, classes.astype(jnp.float32), precision=lax.Precision.HIGHEST),
        hot_cols.T,
        precision=lax.Precision.HIGHEST,
    )
    level_ids = jnp.arange(levels, dtype=jnp.float32)
    tile_rate = jnp.sum(
        (kinds[:, :, None] == level_ids[None, None, :]).astype(jnp.float32) * rates[None, None, :],
        axis=2,
    )
    differ = (atom_rows[:, None] != atom_cols[None, :]).astype(jnp.float32)
    tile_rate = tile_rate * differ
    gamma = expand_mask(tile_rate, TILE, jnp.float32)
    p_rows_out = lax.dynamic_slice_in_dim(p_local, layer * out_rows, out_rows, 1).astype(
        jnp.float32
    )
    real_out = z_imag - gamma * p_rows_out[0]
    imag_out = -z_real - gamma * p_rows_out[1]
    return jnp.stack((real_out, imag_out))


def solution(mesh):
    return jax.shard_map(
        body,
        mesh=mesh,
        in_specs=(
            P(None, "row", "col"),
            P(None, "row", "col"),
            P("row", "col"),
            P("row", "col"),
            P(),
            P(),
            P(),
        ),
        out_specs=P(None, ("row", "depth"), "col"),
        check_vma=False,
    )
```

profile of v0, /device:TPU:1, one launch (start us, length us, event | category | flops | bytes accessed | tf_op | source)
XLA Modules:
  0.0 297.6 jit_solution(12796304798766084277)
XLA Ops:
  6.5 0.0 copy-start.5
  6.5 0.0 copy-start.8
  6.5 0.0 copy-start.7
  6.5 0.0 copy-start.6
  6.5 0.0 all-gather.7.cloned.1.call-start
  6.6 0.7 convert_element_type.34
  7.3 0.1 copy.11
  7.4 0.2 broadcast_in_dim.7
  7.6 0.3 convert_element_type.35
  8.0 1.1 broadcast_multiply_fusion
  9.1 0.0 copy-start.2
  9.1 0.8 fusion.40
  9.8 0.0 all-gather.7.cloned.1.call-update
  9.9 0.0 all-gather.5.cloned.1.call-start
  9.9 0.7 convert_element_type.32
  10.6 0.1 copy.10
  10.7 0.2 broadcast_in_dim.6
  10.9 0.3 convert_element_type.33
  11.3 0.0 copy-done.5
  11.3 0.1 broadcast_multiply_fusion.1
  11.3 0.0 copy-start.3
  11.3 0.8 constant_dynamic-slice_fusion.1
  12.1 0.0 all-gather.5.cloned.1.call-update
  12.1 0.0 all-gather.11.cloned.1.call-start
  12.2 0.0 copy-done.3
  12.2 0.6 all-gather.11.cloned.1.call-update
  12.9 0.0 all-gather.9.cloned.1.call-start
  12.9 0.0 copy-done.2
  12.9 0.5 all-gather.9.cloned.1.call-update
  13.5 0.0 copy-done.8
  13.5 0.1 dynamic_slice.15
  13.5 0.1 dynamic_slice.16
  13.6 0.0 copy-done.7
  13.6 0.2 fusion.30
  13.8 0.2 fusion.33
  14.0 0.0 copy-done.6
  14.0 0.2 select_reduce_fusion
  14.2 0.1 compare_select_fusion
  14.2 0.1 broadcast_in_dim.8
  14.3 0.2 reshape.52
  14.6 68.1 %all-gather.7.cloned.1.call-done = bf16[2,128,4096]{2,1,0:T(8,128)(2,1)} async-done(((bf16[2,128,256]{2,1,0:T(8,128)(2,1)}), bf16[2,128,4096]{2,1,0:T(8,128)(2,1)}) %all-gather.7.cloned.1.call-update) | async-done | bytes 2097168 | tf_op jit(solution)/shard_map/all_gather | solution.py:46
  82.6 2.7 slice_bitcast_fusion.4
  85.3 74.0 %all-gather.5.cloned.1.call-done = bf16[2,128,4096]{2,1,0:T(8,128)(2,1)} async-done(((bf16[2,128,256]{2,1,0:T(8,128)(2,1)}), bf16[2,128,4096]{2,1,0:T(8,128)(2,1)}) %all-gather.5.cloned.1.call-update) | async-done | bytes 2097168 | tf_op jit(solution)/shard_map/all_gather | solution.py:45
  159.4 3.1 %slice_bitcast_fusion.6 = (bf16[128,4096]{1,0:T(8,128)(2,1)}, bf16[128,4096]{1,0:T(8,128)(2,1)}) fusion(bf16[2,128,4096]{2,1,0:T(8,128)(2,1)} %all-gather.5.cloned.1.call-done), kind=kLoop, calls=%fused_computation.31 | loop fusion | bytes 4194304 | tf_op jit(solution)/shard_map/squeeze | solution.py:16
  162.5 46.6 %all-gather.11.cloned.1.call-done = bf16[2,4096,256]{2,1,0:T(8,128)(2,1)} async-done(((bf16[2,512,256]{2,1,0:T(8,128)(2,1)}), bf16[2,4096,256]{2,1,0:T(8,128)(2,1)}) %all-gather.11.cloned.1.call-update) | async-done | bytes 4194320 | tf_op jit(solution)/shard_map/all_gather | solution.py:52
  209.1 0.0 copy-start.1
  209.1 1.9 fusion.39
  210.9 0.9 copy-done.1
  211.9 2.3 slice_bitcast_fusion
  214.1 36.7 %all-gather.9.cloned.1.call-done = bf16[2,4096,256]{2,1,0:T(8,128)(2,1)} async-done(((bf16[2,512,256]{2,1,0:T(8,128)(2,1)}), bf16[2,4096,256]{2,1,0:T(8,128)(2,1)}) %all-gather.9.cloned.1.call-update) | async-done | bytes 4194320 | tf_op jit(solution)/shard_map/all_gather | solution.py:53
  250.8 0.0 copy-start
  250.8 4.6 %slice_bitcast_fusion.1 = (bf16[4096,256]{1,0:T(8,128)(2,1)}, bf16[4096,256]{1,0:T(8,128)(2,1)}) fusion(bf16[2,4096,256]{2,1,0:T(8,128)(2,1)} %all-gather.9.cloned.1.call-done), kind=kLoop, calls=%fused_computation.26 | loop fusion | bytes 8388608 | tf_op jit(solution)/shard_map/squeeze | solution.py:19
  255.4 0.0 copy-done
  255.4 0.0 copy-start.4
  255.4 1.4 fusion.38
  256.8 0.2 copy-done.4
  257.0 33.2 %fusion = f32[128,512]{1,0:T(8,128)S(1)} fusion(bf16[4096,256]{1,0:T(8,128)(2,1)} %get-tuple-element.10, bf16[4096,256]{1,0:T(8,128)(2,1)} %get-tuple-element.9, bf16[4096,256]{1,0:T(8,128)(2,1)S(1)} %fusion.39, bf16[4096,256]{1,0:T(8,128)(2,1)} %get-tuple-element.8, bf16[4096,256]{1,0:T(8,128)(2,1)} %fusion.38, bf16[4096,256]{1,0:T(8,128)(2,1)} %get-tuple-element.7, ...), kind=kOutput, calls=%fused_computation | convolution fusion | flops 2298478592 | bytes 17039360 | tf_op jit(solution)/shard_map/dot_general | solution.py:26
  290.3 0.7 pad_maximum_fusion
  (1 shorter events, 0.0 us)
Async XLA Ops:
  6.5 4.7 %copy-start.5 = (bf16[2,512,256]{2,1,0:T(8,128)(2,1)S(1)}, bf16[2,512,256]{2,1,0:T(8,128)(2,1)}, u32[]{:S(2)}) copy-start(bf16[2,512,256]{2,1,0:T(8,128)(2,1)} %param.7) | copy-start | bytes 1572868
  6.5 6.9 %copy-start.8 = (s32[64]{0:T(128)S(1)}, s32[64]{0:T(128)}, u32[]{:S(2)}) copy-start(s32[64]{0:T(128)} %param.11) | copy-start | bytes 772
  6.5 7.1 %copy-start.7 = (s32[16,16]{1,0:T(8,128)S(1)}, s32[16,16]{1,0:T(8,128)}, u32[]{:S(2)}) copy-start(s32[16,16]{1,0:T(8,128)} %param.12) | copy-start | bytes 3076
  6.5 7.5 %copy-start.6 = (f32[4]{0:T(128)S(1)}, f32[4]{0:T(128)}, u32[]{:S(2)}) copy-start(f32[4]{0:T(128)} %param.13) | copy-start | bytes 52
  6.5 76.1 %all-gather.7.cloned.1.call-start = ((), (), s32[]{:S(2)}) async-start(), calls=%async_computation.1 | async-start | bytes 2228224 | tf_op jit(solution)/shard_map/all_gather | solution.py:46
  9.1 3.8 %copy-start.2 = (bf16[2,512,256]{2,1,0:T(8,128)(2,1)}, bf16[2,512,256]{2,1,0:T(8,128)(2,1)S(1)}, u32[]{:S(2)}) copy-start(bf16[2,512,256]{2,1,0:T(8,128)(2,1)S(1)} %broadcast_multiply_fusion) | copy-start | bytes 1572868
  9.9 149.5 %all-gather.5.cloned.1.call-start = ((), (), s32[]{:S(2)}) async-start(), calls=%async_computation | async-start | bytes 2228224 | tf_op jit(solution)/shard_map/all_gather | solution.py:45
  11.3 0.9 copy-start.3
  12.1 196.9 %all-gather.11.cloned.1.call-start = ((), (), s32[]{:S(2)}) async-start(), calls=%async_computation.3 | async-start | bytes 4718592 | tf_op jit(solution)/shard_map/all_gather | solution.py:52
  12.9 237.9 %all-gather.9.cloned.1.call-start = ((), (), s32[]{:S(2)}) async-start(), calls=%async_computation.2 | async-start | bytes 4718592 | tf_op jit(solution)/shard_map/all_gather | solution.py:53
  209.1 2.8 copy-start.1
  250.8 4.6 %copy-start = (bf16[2,4096,256]{2,1,0:T(8,128)(2,1)S(1)}, bf16[2,4096,256]{2,1,0:T(8,128)(2,1)}, u32[]{:S(2)}) copy-start(bf16[2,4096,256]{2,1,0:T(8,128)(2,1)} %all-gather.9.cloned.1.call-done) | copy-start | bytes 12582916
  255.4 1.6 copy-start.4
Sparse Core Ops, SparseCore 0:
  10.0 72.5 all-gather.6
  84.6 74.7 all-gather.4
  161.5 47.5 all-gather.10
  211.0 39.7 all-gather.8
where the time goes:
time: 298 us
  waiting for transfers between devices  227 us (76%)
  matrix products  33.6 us (11%)
  local copies, waits for them, and re-layouts  14.1 us (5%)
  between operations  13.3 us (4%)
  other arithmetic  9.92 us (3%)
    all_gather x1, waiting for transfers between devices, body(): lax.all_gather(k_strip, 'col', axis=2, tiled=True)  74 us
    all_gather x1, waiting for transfers between devices, body(): lax.all_gather(p_strip, 'col', axis=2, tiled=True)  68.1 us
    all_gather x1, waiting for transfers between devices, body(): lax.all_gather(k_local, 'row', axis=1, tiled=True)  46.6 us
    all_gather x1, waiting for transfers between devices, body(): lax.all_gather(p_local, 'row', axis=1, tiled=True)  36.7 us
    dot_general x1, matrix products, commute(): return jnp.dot(left, right, preferred_element_type=jnp.float32)  33.2 us
  transfers between devices with their start and end apart: 4, of which 4 were waited for; matrix products, arithmetic and copies ran while one was open for 4% of the time, Pallas kernels for 0%

commit v1 on v0

v1 whole, which is shorter than its diff:
```python
import functools

import jax
import jax.numpy as jnp
from jax import lax
from jax.experimental import pallas as pl
from jax.experimental.pallas import tpu as pltpu
from jax.sharding import PartitionSpec as P

TILE = 64
MESH = pl.DeviceIdType.MESH


def expand_mask(mask, tile, dtype):
    rows_t, cols_t = mask.shape
    grid = jnp.broadcast_to(mask[:, None, :, None], (rows_t, tile, cols_t, tile))
    return grid.reshape(rows_t * tile, cols_t * tile).astype(dtype)


def rcopy(src, dst, send_sem, recv_sem, device):
    return pltpu.make_async_remote_copy(
        src_ref=src,
        dst_ref=dst,
        send_sem=send_sem,
        recv_sem=recv_sem,
        device_id=device,
        device_id_type=MESH,
    )


def kernel(
    nr, nz, nd,
    k_ref, p_ref, atoms_ref, classes_ref, rates_ref,
    out_ref,
    cols, rows, acc, zs, zr, xs, xr, ds, dr, ls,
):
    r = lax.axis_index("row")
    z = lax.axis_index("col")
    d = lax.axis_index("depth")
    x = r // 2
    q = r % 2
    nx = nr // 2
    rows_here, cols_here = k_ref.shape[1], k_ref.shape[2]
    rows_out = rows_here // nd
    per_row = rows_here // cols_here
    half = nz // 2
    own_rows = pl.ds(pl.multiple_of(d * rows_out, rows_out), rows_out)

    def rx(step):
        return 2 * lax.rem(x + (step + nx), nx) + q

    def zz(step):
        return lax.rem(z + (step + nz), nz)

    up_z, down_z = (r, zz(1), d), (r, zz(-1), d)
    up_x, down_x = (rx(1), z, d), (rx(-1), z, d)
    twin = (2 * x + 1 - q, z, d)
    z_to = (up_z, down_z)
    x_to = (up_x, down_x)

    barrier = pltpu.get_barrier_semaphore()
    for peer in (up_z, down_z, up_x, down_x, twin):
        pl.semaphore_signal(barrier, inc=1, device_id=peer, device_id_type=MESH)
    pl.semaphore_wait(barrier, 5)

    own = (k_ref, p_ref)

    def row_part(block, part):
        return rows.at[block, pl.ds(2 * part, 2)]

    def col_part(block, part):
        return cols.at[block, pl.ds(2 * (1 - part), 2)]

    def z_copy(way, dist, part):
        block = zz(1 - dist) if way == 0 else zz(dist - 1)
        src = own[part].at[:, own_rows, :] if dist == 1 else row_part(block, part)
        return rcopy(
            src, row_part(block, part), zs.at[way, dist - 1, part],
            zr.at[way, dist - 1, part], z_to[way],
        )

    def z_arrival(way, dist, part):
        block = zz(-dist) if way == 0 else zz(dist)
        slot = row_part(block, part)
        return rcopy(
            slot, slot, zs.at[way, dist - 1, part], zr.at[way, dist - 1, part], z_to[way]
        )

    def z_has(way, dist, part):
        return dist < half or (dist == half and part == way)

    def x_copy(way, idx):
        part = way if idx != 1 else 1 - way
        block = rx(0) if idx < 2 else (rx(-1) if way == 0 else rx(1))
        src = own[part] if idx < 2 else col_part(block, part)
        return rcopy(src, col_part(block, part), xs.at[way, idx], xr.at[way, idx], x_to[way])

    def x_arrival(way, idx):
        part = way if idx != 1 else 1 - way
        step = 1 if idx < 2 else 2
        block = rx(-step) if way == 0 else rx(step)
        slot = col_part(block, part)
        return rcopy(slot, slot, xs.at[way, idx], xr.at[way, idx], x_to[way]), block, part

    def twin_copy(sem, block, part, local):
        src = own[part] if local else col_part(block, part)
        return rcopy(src, col_part(block, part), ds.at[sem], dr.at[sem], twin)

    def twin_arrival(sem, block, part):
        other = block + 1 - 2 * q
        slot = col_part(other, part)
        return rcopy(slot, slot, ds.at[sem], dr.at[sem], twin)

    sent = []
    twins = []

    def start(copy):
        copy.start()
        sent.append(copy)

    for part in (0, 1):
        for way in (0, 1):
            start(z_copy(way, 1, part))
    for idx in (0, 1):
        for way in (0, 1):
            start(x_copy(way, idx))
    for part in (0, 1):
        start(twin_copy(part, r, part, True))
        twins.append((part, r, part))
    local = []
    for part in (0, 1):
        local.append(pltpu.make_async_copy(own[part], col_part(r, part), ls.at[part]))
        local.append(
            pltpu.make_async_copy(
                own[part].at[:, own_rows, :], row_part(z, part), ls.at[2 + part]
            )
        )
    for copy in local:
        copy.start()
    acc[...] = jnp.zeros_like(acc)
    for copy in local:
        copy.wait()

    def x_event(idx):
        for way in (0, 1):
            copy, block, part = x_arrival(way, idx)
            copy.wait_recv()
            if idx == 0:
                start(x_copy(way, 2))
            sem = 2 + 2 * idx + way
            start(twin_copy(sem, block, part, False))
            twins.append((sem, block, part))

    def twin_waits():
        for sem, block, part in twins:
            twin_arrival(sem, block, part).wait_recv()
        twins.clear()

    def multiply(block):
        row = rows[block]
        kre, kim, pre, pim = row[0], row[1], row[2], row[3]
        left = jnp.concatenate(
            (
                jnp.concatenate((kre, -kim, -pre, pim), axis=1),
                jnp.concatenate((kim, kre, -pim, -pre), axis=1),
            ),
            axis=0,
        )
        start_row = pl.multiple_of(lax.rem(block, per_row) * cols_here, cols_here)
        right = cols[block // per_row, :, pl.ds(start_row, cols_here), :]
        right = right.reshape(4 * cols_here, cols_here)
        acc[...] += jnp.dot(left, right, preferred_element_type=jnp.float32)

    far = lax.rem(x + nx // 2, nx)

    def is_far(block):
        return block // (per_row * 2) == far

    def near_blocks(first, last):
        def step(o, carry):
            block = lax.rem(z + (nz + first) + o, nz)

            @pl.when(jnp.logical_not(is_far(block)))
            def _():
                multiply(block)

            return carry

        lax.fori_loop(0, last + 1 - first, step, 0)

    for dist in range(1, half):
        for part in (0, 1):
            for way in (0, 1):
                z_arrival(way, dist, part).wait_recv()
                if z_has(way, dist + 1, part):
                    start(z_copy(way, dist + 1, part))
            if dist == half - 2 and part == 0:
                near_blocks(-(half - 3), -2)
            if dist == half - 2 and part == 1:
                near_blocks(-1, 1)
            if dist == half - 1 and part == 0:
                near_blocks(2, half - 3)
        if dist == half - 5:
            x_event(0)
        if dist == half - 3:
            x_event(1)
            twin_waits()
    x_event(2)
    near_blocks(half - 2, half - 1)
    near_blocks(-(half - 1), -(half - 2))
    twin_waits()

    def far_step(o, carry):
        block = lax.rem(z + (half + 1) + o, nz)

        @pl.when(is_far(block))
        def _():
            multiply(block)

        return carry

    lax.fori_loop(0, nz - 1, far_step, 0)
    for way in (0, 1):
        z_arrival(way, half, way).wait_recv()
    multiply(zz(half))

    lane = lax.broadcasted_iota(jnp.int32, (1, cols_here), 1) // TILE
    for i in range(rows_out // TILE):
        atom_row = atoms_ref[(r * rows_here + d * rows_out) // TILE + i]
        gamma = jnp.zeros((1, cols_here), jnp.float32)
        for j in range(cols_here // TILE):
            atom_col = atoms_ref[z * (cols_here // TILE) + j]
            rate = rates_ref[classes_ref[atom_row, atom_col]]
            rate = jnp.where(atom_row != atom_col, rate, 0.0)
            gamma = jnp.where(lane == j, rate, gamma)
        here = pl.ds(pl.multiple_of(d * rows_out + i * TILE, TILE), TILE)
        p_re = p_ref[0, here, :].astype(jnp.float32)
        p_im = p_ref[1, here, :].astype(jnp.float32)
        z_re = acc[pl.ds(i * TILE, TILE), :]
        z_im = acc[pl.ds(rows_out + i * TILE, TILE), :]
        out_ref[0, pl.ds(i * TILE, TILE), :] = z_im - gamma * p_re
        out_ref[1, pl.ds(i * TILE, TILE), :] = -z_re - gamma * p_im

    for copy in sent:
        copy.wait_send()


def solution(mesh):
    nr, nz, nd = mesh.shape["row"], mesh.shape["col"], mesh.shape["depth"]

    def body(k_parts, p_parts, k_mask, p_mask, atoms, classes, rates):
        k_local = k_parts * expand_mask(k_mask, TILE, jnp.bfloat16)[None]
        p_local = p_parts * expand_mask(p_mask, TILE, jnp.bfloat16)[None]
        rows_here, cols_here = k_local.shape[1:]
        rows_out = rows_here // nd
        half = nz // 2
        return pl.pallas_call(
            functools.partial(kernel, nr, nz, nd),
            out_shape=jax.ShapeDtypeStruct((2, rows_out, cols_here), jnp.float32),
            in_specs=[pl.BlockSpec(memory_space=pltpu.VMEM)] * 2
            + [pl.BlockSpec(memory_space=pltpu.SMEM)] * 3,
            out_specs=pl.BlockSpec(memory_space=pltpu.VMEM),
            scratch_shapes=[
                pltpu.VMEM((nr, 4, rows_here, cols_here), jnp.bfloat16),
                pltpu.VMEM((nz, 4, rows_out, cols_here), jnp.bfloat16),
                pltpu.VMEM((2 * rows_out, cols_here), jnp.float32),
                pltpu.SemaphoreType.DMA((2, half, 2)),
                pltpu.SemaphoreType.DMA((2, half, 2)),
                pltpu.SemaphoreType.DMA((2, 3)),
                pltpu.SemaphoreType.DMA((2, 3)),
                pltpu.SemaphoreType.DMA((8,)),
                pltpu.SemaphoreType.DMA((8,)),
                pltpu.SemaphoreType.DMA((4,)),
            ],
            compiler_params=pltpu.CompilerParams(
                collective_id=0, has_side_effects=True, vmem_limit_bytes=40 * 2**20
            ),
        )(k_local, p_local, atoms, classes, rates)

    return jax.shard_map(
        body,
        mesh=mesh,
        in_specs=(
            P(None, "row", "col"),
            P(None, "row", "col"),
            P("row", "col"),
            P("row", "col"),
            P(),
            P(),
            P(),
        ),
        out_specs=P(None, ("row", "depth"), "col"),
        check_vma=False,
    )
```

time: 298 us -> 65.6 us (0.22)
  waiting for transfers between devices: 227 us -> 0 us
  Pallas kernels: 0 us -> 60.6 us
  matrix products: 33.6 us -> 0 us
  between operations: 13.3 us -> 0.08 us
  local copies, waits for them, and re-layouts: 14.1 us -> 3.95 us
  other arithmetic: 9.92 us -> 0.79 us
    all_gather x4 -> x0, waiting for transfers between devices: 225 us -> none  [the longest x1 74 us: body(): lax.all_gather(k_strip, 'col', axis=2, tiled=True)]
    pallas_call x0 -> x1, Pallas kernels: none -> 60.6 us  [body(): pl.pallas_call(functools.partial(kernel, nr, nz, nd), out_shape=jax.Shape...]
    dot_general x3 -> x0, matrix products: 33.6 us -> none  [the longest x1 33.2 us: commute(): return jnp.dot(left, right, preferred_element_type=jnp.float32)]
    squeeze x3 -> x0, local copies, waits for them, and re-layouts: 10.4 us -> none  [the longest x2 5.81 us: commute(): left = jnp.concatenate((k_rows[0], k_rows[1], p_rows[0], p_rows[1]), axis=1)]
    neg x2 -> x0, other arithmetic: 3.32 us -> none  [the longest x1 1.88 us: commute(): -k_cols[1]]
  transfers between devices with their start and end apart: 4 -> 0, of which waited for: 4 -> 0; matrix products, arithmetic and copies ran while one was open for 4% -> 0% of each run, Pallas kernels for 0% -> 0%
where the time goes in v1:
time: 65.6 us; the launch traced here: 65.4 us
  Pallas kernels  60.6 us (92%)
  local copies, waits for them, and re-layouts  3.95 us (6%)
  other arithmetic  0.79 us (1%)
    pallas_call x1, Pallas kernels, body(): pl.pallas_call(functools.partial(kernel, nr, nz, nd), out_shape=jax.Shape...  60.6 us
    unnamed x13, local copies, waits for them, and re-layouts  2.69 us

profile of v1, /device:TPU:1, one launch (start us, length us, event | category | flops | bytes accessed | tf_op | source)
XLA Modules:
  0.0 65.4 jit_solution(6643216997309587161)
XLA Ops:
  0.0 0.7 %convert_element_type.22 = bf16[8,4]{0,1:T(4,128)(2,1)S(1)} convert(s32[8,4]{0,1:T(4,128)} %param.9) | non-fusion elementwise | flops 32 | bytes 192 | tf_op jit(solution)/shard_map/convert_element_type | solution.py:17
  0.7 0.0 copy-start.5
  0.7 0.1 copy.8
  0.8 0.6 copy-done.5
  1.4 0.1 copy.9
  1.5 0.2 broadcast_in_dim.5
  1.7 0.3 convert_element_type.25
  2.0 0.0 copy-start.4
  2.0 0.2 broadcast_in_dim.4
  2.2 0.0 copy-start.3
  2.3 0.3 convert_element_type.23
  2.6 0.5 copy-done.4
  3.1 0.3 copy-done.3
  3.3 0.0 copy-start
  3.3 0.1 broadcast_multiply_fusion
  3.4 0.0 copy-start.1
  3.5 0.0 copy-start.2
  3.5 0.6 copy-done
  4.0 0.1 copy-done.1
  4.1 0.0 copy-done.2
  4.1 60.6 %shard_map.73 = f32[2,128,256]{2,1,0:T(8,128)S(1)} custom-call(bf16[2,512,256]{2,1,0:T(8,128)(2,1)S(1)} %get-tuple-element.6.k_ref, bf16[2,512,256]{2,1,0:T(8,128)(2,1)S(1)} %get-tuple-element.5.p_ref, s32[64]{0:T(128)S(1)} %copy-done.1, s32[16,16]{1,0:T(8,128)S(1)} %copy-done, f32[4]{0:T(128)S(1)} %copy-done.2), custom_call_target="tpu_custom_call" | custom-call | tf_op jit(solution)/shard_map/pallas_call | solution.py:257
  64.7 0.7 %copy.11 = f32[2,128,256]{2,1,0:T(8,128)} copy(f32[2,128,256]{2,1,0:T(8,128)S(1)} %shard_map.73) | data formatting | bytes 524288
  (1 shorter events, 0.0 us)
Async XLA Ops:
  0.7 0.7 %copy-start.5 = (s32[8,4]{0,1:T(4,128)S(1)}, s32[8,4]{0,1:T(4,128)}, u32[]{:S(2)}) copy-start(s32[8,4]{0,1:T(4,128)} %param.10) | copy-start | bytes 388
  2.0 1.0 %copy-start.4 = (bf16[2,512,256]{2,1,0:T(8,128)(2,1)S(1)}, bf16[2,512,256]{2,1,0:T(8,128)(2,1)}, u32[]{:S(2)}) copy-start(bf16[2,512,256]{2,1,0:T(8,128)(2,1)} %param.7) | copy-start | bytes 1572868
  2.2 1.1 %copy-start.3 = (bf16[2,512,256]{2,1,0:T(8,128)(2,1)S(1)}, bf16[2,512,256]{2,1,0:T(8,128)(2,1)}, u32[]{:S(2)}) copy-start(bf16[2,512,256]{2,1,0:T(8,128)(2,1)} %param.8) | copy-start | bytes 1572868
  3.3 0.7 %copy-start = (s32[16,16]{1,0:T(8,128)S(1)}, s32[16,16]{1,0:T(8,128)}, u32[]{:S(2)}) copy-start(s32[16,16]{1,0:T(8,128)} %classes_ref.1) | copy-start | bytes 3076
  3.4 0.7 %copy-start.1 = (s32[64]{0:T(128)S(1)}, s32[64]{0:T(128)}, u32[]{:S(2)}) copy-start(s32[64]{0:T(128)} %atoms_ref.1) | copy-start | bytes 772
  3.5 0.7 %copy-start.2 = (f32[4]{0:T(128)S(1)}, f32[4]{0:T(128)}, u32[]{:S(2)}) copy-start(f32[4]{0:T(128)} %rates_ref.1) | copy-start | bytes 52

commit v2 on v1

--- a/solution.py
+++ b/solution.py
@@ -8,13 +8,8 @@
 from jax.sharding import PartitionSpec as P
 
 TILE = 64
+CHUNKS = 4
 MESH = pl.DeviceIdType.MESH
-
-
-def expand_mask(mask, tile, dtype):
-    rows_t, cols_t = mask.shape
-    grid = jnp.broadcast_to(mask[:, None, :, None], (rows_t, tile, cols_t, tile))
-    return grid.reshape(rows_t * tile, cols_t * tile).astype(dtype)
 
 
 def rcopy(src, dst, send_sem, recv_sem, device):
@@ -30,10 +25,27 @@
 
 def kernel(
     nr, nz, nd,
-    k_ref, p_ref, atoms_ref, classes_ref, rates_ref,
+    k_hbm, p_hbm, k_mask_hbm, p_mask_hbm, atoms_hbm, classes_hbm, rates_hbm,
     out_ref,
-    cols, rows, acc, zs, zr, xs, xr, ds, dr, ls,
+    k_ref, p_ref, k_mask_ref, p_mask_ref, atoms_ref, classes_ref, rates_ref,
+    cols, rows, acc, zs, zr, xs, xr, ds, dr, ls, fs,
 ):
+    fetches = [
+        pltpu.make_async_copy(src, dst, fs.at[i])
+        for i, (src, dst) in enumerate(
+            (
+                (k_mask_hbm, k_mask_ref),
+                (k_hbm, k_ref),
+                (p_mask_hbm, p_mask_ref),
+                (p_hbm, p_ref),
+                (atoms_hbm, atoms_ref),
+                (classes_hbm, classes_ref),
+                (rates_hbm, rates_ref),
+            )
+        )
+    ]
+    for copy in fetches:
+        copy.start()
     r = lax.axis_index("row")
     z = lax.axis_index("col")
     d = lax.axis_index("depth")
@@ -61,19 +73,50 @@
     barrier = pltpu.get_barrier_semaphore()
     for peer in (up_z, down_z, up_x, down_x, twin):
         pl.semaphore_signal(barrier, inc=1, device_id=peer, device_id_type=MESH)
+
+    for copy in fetches:
+        copy.wait()
+    lane = lax.broadcasted_iota(jnp.int32, (1, cols_here), 1) // TILE
+    for raw, mask_ref, comp in ((k_ref, k_mask_ref, 2), (p_ref, p_mask_ref, 0)):
+        for i in range(rows_here // TILE):
+            keep = jnp.zeros((1, cols_here), jnp.float32)
+            for j in range(cols_here // TILE):
+                keep = jnp.where(lane == j, mask_ref[j, i].astype(jnp.float32), keep)
+            keep = keep.astype(jnp.bfloat16)
+            tile = pl.ds(i * TILE, TILE)
+            for c in (0, 1):
+                cols[r, comp + c, tile, :] = raw[c, tile, :] * keep
+
+    gammas = []
+    for i in range(rows_out // TILE):
+        atom_row = atoms_ref[(r * rows_here + d * rows_out) // TILE + i]
+        gamma = jnp.zeros((1, cols_here), jnp.float32)
+        for j in range(cols_here // TILE):
+            atom_col = atoms_ref[z * (cols_here // TILE) + j]
+            rate = rates_ref[classes_ref[atom_row, atom_col]]
+            rate = jnp.where(atom_row != atom_col, rate, 0.0)
+            gamma = jnp.where(lane == j, rate, gamma)
+        gammas.append(gamma)
+    acc[...] = jnp.zeros_like(acc)
+
     pl.semaphore_wait(barrier, 5)
-
-    own = (k_ref, p_ref)
+    own = (cols.at[r, pl.ds(2, 2)], cols.at[r, pl.ds(0, 2)])
+
+    piece = 2 * rows_out // CHUNKS
 
     def row_part(block, part):
-        return rows.at[block, pl.ds(2 * part, 2)]
+        return rows.at[block, pl.ds(2 * (part % 2), 2), pl.ds(part // 2 * piece, piece)]
+
+    def own_part(part):
+        first = pl.multiple_of(d * rows_out + part // 2 * piece, piece)
+        return own[part % 2].at[:, pl.ds(first, piece), :]
 
     def col_part(block, part):
         return cols.at[block, pl.ds(2 * (1 - part), 2)]
 
     def z_copy(way, dist, part):
         block = zz(1 - dist) if way == 0 else zz(dist - 1)
-        src = own[part].at[:, own_rows, :] if dist == 1 else row_part(block, part)
+        src = own_part(part) if dist == 1 else row_part(block, part)
         return rcopy(
             src, row_part(block, part), zs.at[way, dist - 1, part],
             zr.at[way, dist - 1, part], z_to[way],
@@ -87,7 +130,7 @@
         )
 
     def z_has(way, dist, part):
-        return dist < half or (dist == half and part == way)
+        return dist < half or (dist == half and part % 2 == way)
 
     def x_copy(way, idx):
         part = way if idx != 1 else 1 - way
@@ -118,7 +161,7 @@
         copy.start()
         sent.append(copy)
 
-    for part in (0, 1):
+    for part in range(CHUNKS):
         for way in (0, 1):
             start(z_copy(way, 1, part))
     for idx in (0, 1):
@@ -129,15 +172,13 @@
         twins.append((part, r, part))
     local = []
     for part in (0, 1):
-        local.append(pltpu.make_async_copy(own[part], col_part(r, part), ls.at[part]))
         local.append(
             pltpu.make_async_copy(
-                own[part].at[:, own_rows, :], row_part(z, part), ls.at[2 + part]
+                own[part].at[:, own_rows, :], rows.at[z, pl.ds(2 * part, 2)], ls.at[part]
             )
         )
     for copy in local:
         copy.start()
-    acc[...] = jnp.zeros_like(acc)
     for copy in local:
         copy.wait()
 
@@ -189,16 +230,16 @@
         lax.fori_loop(0, last + 1 - first, step, 0)
 
     for dist in range(1, half):
-        for part in (0, 1):
+        for part in range(CHUNKS):
             for way in (0, 1):
                 z_arrival(way, dist, part).wait_recv()
                 if z_has(way, dist + 1, part):
                     start(z_copy(way, dist + 1, part))
-            if dist == half - 2 and part == 0:
+            if dist == half - 2 and part == CHUNKS // 2 - 1:
                 near_blocks(-(half - 3), -2)
-            if dist == half - 2 and part == 1:
+            if dist == half - 2 and part == CHUNKS - 1:
                 near_blocks(-1, 1)
-            if dist == half - 1 and part == 0:
+            if dist == half - 1 and part == CHUNKS // 2 - 1:
                 near_blocks(2, half - 3)
         if dist == half - 5:
             x_event(0)
@@ -220,26 +261,18 @@
         return carry
 
     lax.fori_loop(0, nz - 1, far_step, 0)
-    for way in (0, 1):
-        z_arrival(way, half, way).wait_recv()
+    for part in range(CHUNKS):
+        z_arrival(part % 2, half, part).wait_recv()
     multiply(zz(half))
 
-    lane = lax.broadcasted_iota(jnp.int32, (1, cols_here), 1) // TILE
     for i in range(rows_out // TILE):
-        atom_row = atoms_ref[(r * rows_here + d * rows_out) // TILE + i]
-        gamma = jnp.zeros((1, cols_here), jnp.float32)
-        for j in range(cols_here // TILE):
-            atom_col = atoms_ref[z * (cols_here // TILE) + j]
-            rate = rates_ref[classes_ref[atom_row, atom_col]]
-            rate = jnp.where(atom_row != atom_col, rate, 0.0)
-            gamma = jnp.where(lane == j, rate, gamma)
-        here = pl.ds(pl.multiple_of(d * rows_out + i * TILE, TILE), TILE)
-        p_re = p_ref[0, here, :].astype(jnp.float32)
-        p_im = p_ref[1, here, :].astype(jnp.float32)
-        z_re = acc[pl.ds(i * TILE, TILE), :]
+        tile = pl.ds(i * TILE, TILE)
+        p_re = rows[z, 2, tile, :].astype(jnp.float32)
+        p_im = rows[z, 3, tile, :].astype(jnp.float32)
+        z_re = acc[tile, :]
         z_im = acc[pl.ds(rows_out + i * TILE, TILE), :]
-        out_ref[0, pl.ds(i * TILE, TILE), :] = z_im - gamma * p_re
-        out_ref[1, pl.ds(i * TILE, TILE), :] = -z_re - gamma * p_im
+        out_ref[0, tile, :] = z_im - gammas[i] * p_re
+        out_ref[1, tile, :] = -z_re - gammas[i] * p_im
 
     for copy in sent:
         copy.wait_send()
@@ -249,33 +282,38 @@
     nr, nz, nd = mesh.shape["row"], mesh.shape["col"], mesh.shape["depth"]
 
     def body(k_parts, p_parts, k_mask, p_mask, atoms, classes, rates):
-        k_local = k_parts * expand_mask(k_mask, TILE, jnp.bfloat16)[None]
-        p_local = p_parts * expand_mask(p_mask, TILE, jnp.bfloat16)[None]
-        rows_here, cols_here = k_local.shape[1:]
+        rows_here, cols_here = k_parts.shape[1:]
         rows_out = rows_here // nd
         half = nz // 2
         return pl.pallas_call(
             functools.partial(kernel, nr, nz, nd),
             out_shape=jax.ShapeDtypeStruct((2, rows_out, cols_here), jnp.float32),
-            in_specs=[pl.BlockSpec(memory_space=pltpu.VMEM)] * 2
-            + [pl.BlockSpec(memory_space=pltpu.SMEM)] * 3,
+            in_specs=[pl.BlockSpec(memory_space=pltpu.HBM)] * 7,
             out_specs=pl.BlockSpec(memory_space=pltpu.VMEM),
             scratch_shapes=[
+                pltpu.VMEM(k_parts.shape, k_parts.dtype),
+                pltpu.VMEM(p_parts.shape, p_parts.dtype),
+                pltpu.SMEM(k_mask.T.shape, k_mask.dtype),
+                pltpu.SMEM(p_mask.T.shape, p_mask.dtype),
+                pltpu.SMEM(atoms.shape, atoms.dtype),
+                pltpu.SMEM(classes.shape, classes.dtype),
+                pltpu.SMEM(rates.shape, rates.dtype),
                 pltpu.VMEM((nr, 4, rows_here, cols_here), jnp.bfloat16),
                 pltpu.VMEM((nz, 4, rows_out, cols_here), jnp.bfloat16),
                 pltpu.VMEM((2 * rows_out, cols_here), jnp.float32),
-                pltpu.SemaphoreType.DMA((2, half, 2)),
-                pltpu.SemaphoreType.DMA((2, half, 2)),
+                pltpu.SemaphoreType.DMA((2, half, CHUNKS)),
+                pltpu.SemaphoreType.DMA((2, half, CHUNKS)),
                 pltpu.SemaphoreType.DMA((2, 3)),
                 pltpu.SemaphoreType.DMA((2, 3)),
                 pltpu.SemaphoreType.DMA((8,)),
                 pltpu.SemaphoreType.DMA((8,)),
-                pltpu.SemaphoreType.DMA((4,)),
+                pltpu.SemaphoreType.DMA((2,)),
+                pltpu.SemaphoreType.DMA((7,)),
             ],
             compiler_params=pltpu.CompilerParams(
-                collective_id=0, has_side_effects=True, vmem_limit_bytes=40 * 2**20
+                collective_id=0, has_side_effects=True, vmem_limit_bytes=67_043_328
             ),
-        )(k_local, p_local, atoms, classes, rates)
+        )(k_parts, p_parts, k_mask.T, p_mask.T, atoms, classes, rates)
 
     return jax.shard_map(
         body,

time: 65.6 us -> 62 us (0.945)
  local copies, waits for them, and re-layouts: 3.95 us -> 1.67 us
  other arithmetic: 0.79 us -> 0 us
    unnamed x13 -> x1, local copies, waits for them, and re-layouts: 2.69 us -> 1.67 us
    convert_element_type x4 -> x0, local copies, waits for them, and re-layouts: 0.86 us -> none  [expand_mask(): return grid.reshape(rows_t * tile, cols_t * tile).astype(dtype)]
    convert_element_type x2 -> x0, other arithmetic: 0.69 us -> none  [expand_mask(): return grid.reshape(rows_t * tile, cols_t * tile).astype(dtype)]
where the time goes in v2:
time: 62 us; the launch traced here: 61.8 us
  Pallas kernels  60.1 us (97%)
  local copies, waits for them, and re-layouts  1.67 us (3%)
    pallas_call x1, Pallas kernels, body(): pl.pallas_call(functools.partial(kernel, nr, nz, nd), out_shape=jax.Shape...  60.1 us
    unnamed x1, local copies, waits for them, and re-layouts  1.67 us

profile of v2, /device:TPU:1, one launch (start us, length us, event | category | flops | bytes accessed | tf_op | source)
XLA Modules:
  0.0 61.8 jit_solution(12586340703442056353)
XLA Ops:
  0.0 60.1 %shard_map.73 = f32[2,128,256]{2,1,0:T(8,128)} custom-call(bf16[2,512,256]{2,1,0:T(8,128)(2,1)} %k_hbm.1, bf16[2,512,256]{2,1,0:T(8,128)(2,1)} %p_hbm.1, s32[4,8]{1,0:T(4,128)} %bitcast.2, s32[4,8]{1,0:T(4,128)} %bitcast.3, s32[64]{0:T(128)} %atoms_hbm.1, s32[16,16]{1,0:T(8,128)} %classes_hbm.1, f32[4]{0:T(128)} %rates_hbm.1), custom_call_target="tpu_custom_call" | custom-call | tf_op jit(solution)/shard_map/pallas_call | solution.py:288
  60.1 1.7 %copy.9 = f32[2,128,256]{2,1,0:T(8,128)} copy(f32[2,128,256]{2,1,0:T(8,128)} %shard_map.73) | data formatting | bytes 524288

commit v3 on v2

--- a/solution.py
+++ b/solution.py
@@ -28,7 +28,7 @@
     k_hbm, p_hbm, k_mask_hbm, p_mask_hbm, atoms_hbm, classes_hbm, rates_hbm,
     out_ref,
     k_ref, p_ref, k_mask_ref, p_mask_ref, atoms_ref, classes_ref, rates_ref,
-    cols, rows, acc, zs, zr, xs, xr, ds, dr, ls, fs,
+    cols, rows, acc, zs, zr, xs, xr, ys, yr, ds, dr, ls, fs,
 ):
     fetches = [
         pltpu.make_async_copy(src, dst, fs.at[i])
@@ -69,9 +69,11 @@
     twin = (2 * x + 1 - q, z, d)
     z_to = (up_z, down_z)
     x_to = (up_x, down_x)
+    up_y, down_y = (r, z, lax.rem(d + 1, nd)), (r, z, lax.rem(d + nd - 1, nd))
+    y_to = (up_y, down_y)
 
     barrier = pltpu.get_barrier_semaphore()
-    for peer in (up_z, down_z, up_x, down_x, twin):
+    for peer in (up_z, down_z, up_x, down_x, up_y, down_y, twin):
         pl.semaphore_signal(barrier, inc=1, device_id=peer, device_id_type=MESH)
 
     for copy in fetches:
@@ -99,7 +101,7 @@
         gammas.append(gamma)
     acc[...] = jnp.zeros_like(acc)
 
-    pl.semaphore_wait(barrier, 5)
+    pl.semaphore_wait(barrier, 7)
     own = (cols.at[r, pl.ds(2, 2)], cols.at[r, pl.ds(0, 2)])
 
     piece = 2 * rows_out // CHUNKS
@@ -132,27 +134,42 @@
     def z_has(way, dist, part):
         return dist < half or (dist == half and part % 2 == way)
 
+    def quarter(block, turn):
+        first = lax.rem(d + (turn + nd), nd) * rows_out
+        return cols.at[block, :, pl.ds(pl.multiple_of(first, rows_out), rows_out), :]
+
+    def x_turn(way, idx):
+        return (0, nd // 2)[way if idx == 2 else idx]
+
     def x_copy(way, idx):
-        part = way if idx != 1 else 1 - way
-        block = rx(0) if idx < 2 else (rx(-1) if way == 0 else rx(1))
-        src = own[part] if idx < 2 else col_part(block, part)
-        return rcopy(src, col_part(block, part), xs.at[way, idx], xr.at[way, idx], x_to[way])
+        step = 0 if idx < 2 else 1
+        slot = quarter(rx(-step) if way == 0 else rx(step), x_turn(way, idx))
+        return rcopy(slot, slot, xs.at[way, idx], xr.at[way, idx], x_to[way])
 
     def x_arrival(way, idx):
-        part = way if idx != 1 else 1 - way
         step = 1 if idx < 2 else 2
         block = rx(-step) if way == 0 else rx(step)
+        slot = quarter(block, x_turn(way, idx))
+        return rcopy(slot, slot, xs.at[way, idx], xr.at[way, idx], x_to[way]), block
+
+    y_blocks = (rx(-1), rx(1), rx(-2))
+
+    def y_copy(way, j):
+        slot = quarter(y_blocks[j], 0)
+        return rcopy(slot, slot, ys.at[way, j], yr.at[way, j], y_to[way])
+
+    def y_arrival(way, j):
+        slot = quarter(y_blocks[j], -1 if way == 0 else 1)
+        return rcopy(slot, slot, ys.at[way, j], yr.at[way, j], y_to[way])
+
+    def to_twin(sem, block, turn):
+        slot = quarter(block, turn)
+        start(rcopy(slot, slot, ds.at[sem], dr.at[sem], twin))
+        twins.append((sem, block, turn))
+
+    def own_to_twin(part, block):
         slot = col_part(block, part)
-        return rcopy(slot, slot, xs.at[way, idx], xr.at[way, idx], x_to[way]), block, part
-
-    def twin_copy(sem, block, part, local):
-        src = own[part] if local else col_part(block, part)
-        return rcopy(src, col_part(block, part), ds.at[sem], dr.at[sem], twin)
-
-    def twin_arrival(sem, block, part):
-        other = block + 1 - 2 * q
-        slot = col_part(other, part)
-        return rcopy(slot, slot, ds.at[sem], dr.at[sem], twin)
+        return rcopy(slot, slot, ds.at[part], dr.at[part], twin)
 
     sent = []
     twins = []
@@ -168,8 +185,7 @@
         for way in (0, 1):
             start(x_copy(way, idx))
     for part in (0, 1):
-        start(twin_copy(part, r, part, True))
-        twins.append((part, r, part))
+        start(own_to_twin(part, r))
     local = []
     for part in (0, 1):
         local.append(
@@ -184,18 +200,27 @@
 
     def x_event(idx):
         for way in (0, 1):
-            copy, block, part = x_arrival(way, idx)
+            copy, block = x_arrival(way, idx)
             copy.wait_recv()
-            if idx == 0:
+            if idx < 2 and idx == way:
                 start(x_copy(way, 2))
-            sem = 2 + 2 * idx + way
-            start(twin_copy(sem, block, part, False))
-            twins.append((sem, block, part))
+            if x_turn(way, idx) == 0:
+                j = 2 if idx == 2 else way
+                for y_way in (0, 1):
+                    start(y_copy(y_way, j))
+            to_twin(2 + 2 * idx + way, block, x_turn(way, idx))
+
+    def y_event(j):
+        for way in (0, 1):
+            y_arrival(way, j).wait_recv()
+            to_twin(8 + 2 * j + way, y_blocks[j], -1 if way == 0 else 1)
 
     def twin_waits():
-        for sem, block, part in twins:
-            twin_arrival(sem, block, part).wait_recv()
-        twins.clear()
+        for part in (0, 1):
+            own_to_twin(part, r + 1 - 2 * q).wait_recv()
+        for sem, block, turn in twins:
+            slot = quarter(block + 1 - 2 * q, turn)
+            rcopy(slot, slot, ds.at[sem], dr.at[sem], twin).wait_recv()
 
     def multiply(block):
         row = rows[block]
@@ -212,55 +237,35 @@
         right = right.reshape(4 * cols_here, cols_here)
         acc[...] += jnp.dot(left, right, preferred_element_type=jnp.float32)
 
-    far = lax.rem(x + nx // 2, nx)
-
-    def is_far(block):
-        return block // (per_row * 2) == far
-
-    def near_blocks(first, last):
+    def blocks(first, last):
         def step(o, carry):
-            block = lax.rem(z + (nz + first) + o, nz)
-
-            @pl.when(jnp.logical_not(is_far(block)))
-            def _():
-                multiply(block)
-
+            multiply(lax.rem(z + (nz + first) + o, nz))
             return carry
 
         lax.fori_loop(0, last + 1 - first, step, 0)
 
+    events = {
+        (2, 0): lambda: x_event(0),
+        (3, 0): lambda: x_event(1),
+        (4, 0): lambda: x_event(2),
+        (4, 2): lambda: (y_event(0), y_event(1)),
+        (5, 3): lambda: y_event(2),
+        (6, 0): twin_waits,
+        (6, 1): lambda: blocks(-5, -4),
+        (6, 2): lambda: blocks(-3, -2),
+        (6, 3): lambda: blocks(-1, 1),
+        (7, 0): lambda: blocks(2, 3),
+        (7, 1): lambda: blocks(4, 5),
+    }
     for dist in range(1, half):
         for part in range(CHUNKS):
             for way in (0, 1):
                 z_arrival(way, dist, part).wait_recv()
                 if z_has(way, dist + 1, part):
                     start(z_copy(way, dist + 1, part))
-            if dist == half - 2 and part == CHUNKS // 2 - 1:
-                near_blocks(-(half - 3), -2)
-            if dist == half - 2 and part == CHUNKS - 1:
-                near_blocks(-1, 1)
-            if dist == half - 1 and part == CHUNKS // 2 - 1:
-                near_blocks(2, half - 3)
-        if dist == half - 5:
-            x_event(0)
-        if dist == half - 3:
-            x_event(1)
-            twin_waits()
-    x_event(2)
-    near_blocks(half - 2, half - 1)
-    near_blocks(-(half - 1), -(half - 2))
-    twin_waits()
-
-    def far_step(o, carry):
-        block = lax.rem(z + (half + 1) + o, nz)
-
-        @pl.when(is_far(block))
-        def _():
-            multiply(block)
-
-        return carry
-
-    lax.fori_loop(0, nz - 1, far_step, 0)
+            events.get((dist, part), lambda: None)()
+    blocks(6, 7)
+    blocks(-7, -6)
     for part in range(CHUNKS):
         z_arrival(part % 2, half, part).wait_recv()
     multiply(zz(half))
@@ -305,8 +310,10 @@
                 pltpu.SemaphoreType.DMA((2, half, CHUNKS)),
                 pltpu.SemaphoreType.DMA((2, 3)),
                 pltpu.SemaphoreType.DMA((2, 3)),
-                pltpu.SemaphoreType.DMA((8,)),
-                pltpu.SemaphoreType.DMA((8,)),
+                pltpu.SemaphoreType.DMA((2, 3)),
+                pltpu.SemaphoreType.DMA((2, 3)),
+                pltpu.SemaphoreType.DMA((14,)),
+                pltpu.SemaphoreType.DMA((14,)),
                 pltpu.SemaphoreType.DMA((2,)),
                 pltpu.SemaphoreType.DMA((7,)),
             ],

time: 62 us -> 60.6 us (0.977)
  Pallas kernels: 60.1 us -> 58.6 us
    pallas_call x1, Pallas kernels: 60.1 us -> 58.6 us  [body(): pl.pallas_call(functools.partial(kernel, nr, nz, nd), out_shape=jax.Shape...]
where the time goes in v3:
time: 60.6 us; the launch traced here: 60.3 us
  Pallas kernels  58.6 us (97%)
  local copies, waits for them, and re-layouts  1.67 us (3%)
    pallas_call x1, Pallas kernels, body(): pl.pallas_call(functools.partial(kernel, nr, nz, nd), out_shape=jax.Shape...  58.6 us
    unnamed x1, local copies, waits for them, and re-layouts  1.67 us

profile of v3, /device:TPU:1, one launch (start us, length us, event | category | flops | bytes accessed | tf_op | source)
XLA Modules:
  0.0 60.3 jit_solution(3456268442471120310)
XLA Ops:
  0.0 58.6 %shard_map.73 = f32[2,128,256]{2,1,0:T(8,128)} custom-call(bf16[2,512,256]{2,1,0:T(8,128)(2,1)} %k_hbm.1, bf16[2,512,256]{2,1,0:T(8,128)(2,1)} %p_hbm.1, s32[4,8]{1,0:T(4,128)} %bitcast.2, s32[4,8]{1,0:T(4,128)} %bitcast.3, s32[64]{0:T(128)} %atoms_hbm.1, s32[16,16]{1,0:T(8,128)} %classes_hbm.1, f32[4]{0:T(128)} %rates_hbm.1), custom_call_target="tpu_custom_call" | custom-call | tf_op jit(solution)/shard_map/pallas_call | solution.py:293
  58.6 1.7 %copy.9 = f32[2,128,256]{2,1,0:T(8,128)} copy(f32[2,128,256]{2,1,0:T(8,128)} %shard_map.73) | data formatting | bytes 524288

commit v4 on v3

--- a/solution.py
+++ b/solution.py
@@ -318,9 +318,9 @@
                 pltpu.SemaphoreType.DMA((7,)),
             ],
             compiler_params=pltpu.CompilerParams(
-                collective_id=0, has_side_effects=True, vmem_limit_bytes=67_043_328
+                collective_id=0, has_side_effects=True, vmem_limit_bytes=40 * 2**20
             ),
-        )(k_parts, p_parts, k_mask.T, p_mask.T, atoms, classes, rates)
+        )(*(pltpu.with_memory_space_constraint(v, pltpu.HBM) for v in (k_parts, p_parts, k_mask.T, p_mask.T, atoms, classes, rates)))
 
     return jax.shard_map(
         body,

time: 60.6 us -> 59 us (0.974)
  local copies, waits for them, and re-layouts: 1.67 us -> 0.71 us
  Pallas kernels: 58.6 us -> 57.9 us
    unnamed x1, local copies, waits for them, and re-layouts: 1.67 us -> 0.71 us
    pallas_call x1, Pallas kernels: 58.6 us -> 57.9 us  [body(): pl.pallas_call(functools.partial(kernel, nr, nz, nd), out_shape=jax.Shape...]
where the time goes in v4:
time: 59 us; the launch traced here: 58.6 us
  Pallas kernels  57.9 us (98%)
  local copies, waits for them, and re-layouts  0.71 us (1%)
    pallas_call x1, Pallas kernels, body(): pl.pallas_call(functools.partial(kernel, nr, nz, nd), out_shape=jax.Shape...  57.9 us

profile of v4, /device:TPU:1, one launch (start us, length us, event | category | flops | bytes accessed | tf_op | source)
XLA Modules:
  0.0 58.6 jit_solution(5074821807189708796)
XLA Ops:
  0.0 57.9 %shard_map.73 = f32[2,128,256]{2,1,0:T(8,128)S(1)} custom-call(bf16[2,512,256]{2,1,0:T(8,128)(2,1)} %k_hbm.1, bf16[2,512,256]{2,1,0:T(8,128)(2,1)} %p_hbm.1, s32[4,8]{1,0:T(4,128)} %bitcast.2, s32[4,8]{1,0:T(4,128)} %bitcast.3, s32[64]{0:T(128)} %atoms_hbm.1, s32[16,16]{1,0:T(8,128)} %classes_hbm.1, f32[4]{0:T(128)} %rates_hbm.1), custom_call_target="tpu_custom_call" | custom-call | tf_op jit(solution)/shard_map/pallas_call | solution.py:293
  57.9 0.7 %copy.9 = f32[2,128,256]{2,1,0:T(8,128)} copy(f32[2,128,256]{2,1,0:T(8,128)S(1)} %shard_map.73) | data formatting | bytes 524288

commit v5 on v4

--- a/solution.py
+++ b/solution.py
@@ -131,8 +131,16 @@
             slot, slot, zs.at[way, dist - 1, part], zr.at[way, dist - 1, part], z_to[way]
         )
 
-    def z_has(way, dist, part):
-        return dist < half or (dist == half and part % 2 == way)
+    def comes(way, part, at):
+        if part >= CHUNKS // 2:
+            return way == 1
+        up = part + jnp.maximum(2 - at, 0) < CHUNKS // 2
+        return up if way == 0 else jnp.logical_not(up)
+
+    def opposite(way, part, act):
+        pred = comes(way, part, zz(1) if way == 0 else zz(-1))
+        if pred is not False:
+            pl.when(pred)(lambda: act(z_copy(way, half, part)))
 
     def quarter(block, turn):
         first = lax.rem(d + (turn + nd), nd) * rows_out
@@ -222,20 +230,24 @@
             slot = quarter(block + 1 - 2 * q, turn)
             rcopy(slot, slot, ds.at[sem], dr.at[sem], twin).wait_recv()
 
-    def multiply(block):
-        row = rows[block]
-        kre, kim, pre, pim = row[0], row[1], row[2], row[3]
-        left = jnp.concatenate(
+    def left_of(block, some):
+        kre, kim, pre, pim = (rows[block, comp, some, :] for comp in range(4))
+        return jnp.concatenate(
             (
                 jnp.concatenate((kre, -kim, -pre, pim), axis=1),
                 jnp.concatenate((kim, kre, -pim, -pre), axis=1),
             ),
             axis=0,
         )
+
+    def right_of(block):
         start_row = pl.multiple_of(lax.rem(block, per_row) * cols_here, cols_here)
         right = cols[block // per_row, :, pl.ds(start_row, cols_here), :]
-        right = right.reshape(4 * cols_here, cols_here)
-        acc[...] += jnp.dot(left, right, preferred_element_type=jnp.float32)
+        return right.reshape(4 * cols_here, cols_here)
+
+    def multiply(block):
+        left = left_of(block, pl.ds(0, rows_out))
+        acc[...] += jnp.dot(left, right_of(block), preferred_element_type=jnp.float32)
 
     def blocks(first, last):
         def step(o, carry):
@@ -245,42 +257,50 @@
         lax.fori_loop(0, last + 1 - first, step, 0)
 
     events = {
-        (2, 0): lambda: x_event(0),
-        (3, 0): lambda: x_event(1),
-        (4, 0): lambda: x_event(2),
-        (4, 2): lambda: (y_event(0), y_event(1)),
-        (5, 3): lambda: y_event(2),
-        (6, 0): twin_waits,
-        (6, 1): lambda: blocks(-5, -4),
-        (6, 2): lambda: blocks(-3, -2),
-        (6, 3): lambda: blocks(-1, 1),
-        (7, 0): lambda: blocks(2, 3),
-        (7, 1): lambda: blocks(4, 5),
+        (2, 2): lambda: x_event(0),
+        (3, 2): lambda: x_event(1),
+        (4, 2): lambda: x_event(2),
+        (5, 0): lambda: (y_event(0), y_event(1)),
+        (6, 1): lambda: y_event(2),
+        (6, 2): twin_waits,
+        (6, 3): lambda: blocks(-5, -4),
+        (7, 0): lambda: blocks(-3, -1),
+        (7, 1): lambda: blocks(0, 2),
+        (7, 2): lambda: blocks(3, 5),
     }
     for dist in range(1, half):
         for part in range(CHUNKS):
-            for way in (0, 1):
+            for way in (1, 0):
                 z_arrival(way, dist, part).wait_recv()
-                if z_has(way, dist + 1, part):
+                if dist + 1 < half:
                     start(z_copy(way, dist + 1, part))
+                else:
+                    opposite(way, part, lambda copy: copy.start())
             events.get((dist, part), lambda: None)()
     blocks(6, 7)
     blocks(-7, -6)
-    for part in range(CHUNKS):
-        z_arrival(part % 2, half, part).wait_recv()
-    multiply(zz(half))
-
+    last = zz(half)
+    right = right_of(last)
     for i in range(rows_out // TILE):
         tile = pl.ds(i * TILE, TILE)
+        for part in (2 * i, 2 * i + 1):
+            for way in (0, 1):
+                pred = comes(way, part, z)
+                if pred is not False:
+                    pl.when(pred)(lambda: z_arrival(way, half, part).wait_recv())
+        both = jnp.dot(left_of(last, tile), right, preferred_element_type=jnp.float32)
+        z_re = acc[tile, :] + both[:TILE]
+        z_im = acc[pl.ds(rows_out + i * TILE, TILE), :] + both[TILE:]
         p_re = rows[z, 2, tile, :].astype(jnp.float32)
         p_im = rows[z, 3, tile, :].astype(jnp.float32)
-        z_re = acc[tile, :]
-        z_im = acc[pl.ds(rows_out + i * TILE, TILE), :]
         out_ref[0, tile, :] = z_im - gammas[i] * p_re
         out_ref[1, tile, :] = -z_re - gammas[i] * p_im
 
     for copy in sent:
         copy.wait_send()
+    for part in range(CHUNKS):
+        for way in (0, 1):
+            opposite(way, part, lambda copy: copy.wait_send())
 
 
 def solution(mesh):

time: 59 us -> 58.2 us (0.986)
  Pallas kernels: 57.9 us -> 56.9 us
    pallas_call x1, Pallas kernels: 57.9 us -> 56.9 us  [body(): pl.pallas_call(functools.partial(kernel, nr, nz, nd), out_shape=jax.Shape...]
where the time goes in v5:
time: 58.2 us; the launch traced here: 57.6 us
  Pallas kernels  56.9 us (98%)
  local copies, waits for them, and re-layouts  0.71 us (1%)
    pallas_call x1, Pallas kernels, body(): pl.pallas_call(functools.partial(kernel, nr, nz, nd), out_shape=jax.Shape...  56.9 us

profile of v5, /device:TPU:1, one launch (start us, length us, event | category | flops | bytes accessed | tf_op | source)
XLA Modules:
  0.0 57.6 jit_solution(8984923996421921186)
XLA Ops:
  0.0 56.9 %shard_map.73 = f32[2,128,256]{2,1,0:T(8,128)S(1)} custom-call(bf16[2,512,256]{2,1,0:T(8,128)(2,1)} %k_hbm.1, bf16[2,512,256]{2,1,0:T(8,128)(2,1)} %p_hbm.1, s32[4,8]{1,0:T(4,128)} %bitcast.2, s32[4,8]{1,0:T(4,128)} %bitcast.3, s32[64]{0:T(128)} %atoms_hbm.1, s32[16,16]{1,0:T(8,128)} %classes_hbm.1, f32[4]{0:T(128)} %rates_hbm.1), custom_call_target="tpu_custom_call" | custom-call | tf_op jit(solution)/shard_map/pallas_call | solution.py:313
  56.9 0.7 %copy.9 = f32[2,128,256]{2,1,0:T(8,128)} copy(f32[2,128,256]{2,1,0:T(8,128)S(1)} %shard_map.73) | data formatting | bytes 524288

commit v6 on v5

--- a/solution.py
+++ b/solution.py
@@ -134,7 +134,7 @@
     def comes(way, part, at):
         if part >= CHUNKS // 2:
             return way == 1
-        up = part + jnp.maximum(2 - at, 0) < CHUNKS // 2
+        up = part + jnp.clip(3 - at, 0, 2) < CHUNKS // 2
         return up if way == 0 else jnp.logical_not(up)
 
     def opposite(way, part, act):

time: 58.2 us -> 58 us (level)
  no operation moved by 1% of the time
where the time goes in v6:
time: 58 us; the launch traced here: 57.6 us
  Pallas kernels  56.9 us (98%)
  local copies, waits for them, and re-layouts  0.71 us (1%)
    pallas_call x1, Pallas kernels, body(): pl.pallas_call(functools.partial(kernel, nr, nz, nd), out_shape=jax.Shape...  56.9 us

profile of v6, /device:TPU:1, one launch (start us, length us, event | category | flops | bytes accessed | tf_op | source)
XLA Modules:
  0.0 57.6 jit_solution(2519140154797757380)
XLA Ops:
  0.0 56.9 %shard_map.73 = f32[2,128,256]{2,1,0:T(8,128)S(1)} custom-call(bf16[2,512,256]{2,1,0:T(8,128)(2,1)} %k_hbm.1, bf16[2,512,256]{2,1,0:T(8,128)(2,1)} %p_hbm.1, s32[4,8]{1,0:T(4,128)} %bitcast.2, s32[4,8]{1,0:T(4,128)} %bitcast.3, s32[64]{0:T(128)} %atoms_hbm.1, s32[16,16]{1,0:T(8,128)} %classes_hbm.1, f32[4]{0:T(128)} %rates_hbm.1), custom_call_target="tpu_custom_call" | custom-call | tf_op jit(solution)/shard_map/pallas_call | solution.py:313
  56.9 0.7 %copy.9 = f32[2,128,256]{2,1,0:T(8,128)} copy(f32[2,128,256]{2,1,0:T(8,128)S(1)} %shard_map.73) | data formatting | bytes 524288
